TPU v7x, 32 devices: a whole 2x2x4 slice. The times are simulated.
32 devices in a mesh: swath: 8 (over y, x, core), chan: 4 (over z).
Axes of the slice: x: 2, y: 2, z: 4, core: 2. Of those that a mesh axis runs over, the one named last changes fastest.
Arguments:
- innovations: float32 [524288], P(('swath', 'chan')), may hold values from -6 to 6
- obs_precision: float32 [524288], P(('swath', 'chan')), may hold values from 0.25 to 4
- jacobian: bfloat16 [524288, 128], P(('swath', 'chan')), may hold values from -0.5 to 0.5
- predictors: float32 [8, 524288], P(None, ('swath', 'chan')), may hold values from -5 to 5
- obs_column: int32 [524288], P(('swath', 'chan')), may hold values from 0 to 2047, as said below
- obs_channel: int32 [524288], P(('swath', 'chan')), may hold values from 0 to 5119
- obs_count: int32 [8, 4], P('swath', 'chan'), may hold values from 5461 to 16384, as said below
- smoothing: float32 [128], replicated, may hold values from 0.02 to 0.12
- bias_precision: float32 [8, 5120], P(None, 'chan'), may hold values from 1 to 100
Outputs:
- control_state: float32 [256, 256, 128], P('swath', 'chan')
- bias_increment: float32 [8, 5120], P(None, 'chan')
- residual_norms: float32 [3], replicated
Inputs may be any that keep to these rules, and one draw needn't show every extreme that they name: `obs_column`: Row-major index latitude row * 64 + longitude column within the tile of the device that holds the slot; all slots of an aligned block of 128 slots lie in one latitude row. `obs_channel`: channel c belongs to block c // 256, whose coefficients are owned by chan index c // 1280. `obs_count`: slots below the count hold live observations, the rest are ignored; some device is full in every draw.
All inputs are finite; a program needn't handle non-finite values.
Results may differ from a plain program's by a relative error of at most 0.0003.
Values sent between devices are 32-bit elements; how exact they have to be, the bound alone decides.
A program may use at most 128 MiB of HBM per device.

v0:
```python
import jax
import jax.numpy as jnp
from jax import lax
from jax.sharding import PartitionSpec as P

LEV = 128
NPRED = 8
CH_BLOCK = 256
OBS_BLOCK = 128
LAT_DEV = 32
LON_DEV = 64
ITERS = 2


def with_halo(array, sides, width):
    for axis, dim in sides:
        size, length = (lax.axis_size(axis), array.shape[dim])
        up = [(i, (i + 1) % size) for i in range(size)]
        down = [(j, i) for i, j in up]
        last = lax.slice_in_dim(array, length - width, length, axis=dim)
        leading = lax.slice_in_dim(array, 0, width, axis=dim)
        before = lax.ppermute(last, axis, up)
        after = lax.ppermute(leading, axis, down)
        array = jnp.concatenate([before, array, after], axis=dim)
    return array


def body(
    innovations,
    obs_precision,
    jacobian,
    predictors,
    obs_column,
    obs_channel,
    obs_count,
    smoothing,
    bias_precision,
):
    owned_width = bias_precision.shape[1]
    channels_all = owned_width * lax.axis_size("chan")
    block_ids = channels_all // CH_BLOCK
    slot_total = obs_precision.shape[0]
    line_count = slot_total // OBS_BLOCK
    band_index = lax.axis_index("swath")
    top_keep = band_index > 0
    bottom_keep = band_index < lax.axis_size("swath") - 1
    bias_weight = jnp.where(band_index == 0, 1.0, 0.0).astype(jnp.float32)
    live = jnp.arange(slot_total, dtype=jnp.int32) < obs_count[0, 0]
    weights = jnp.where(live, obs_precision, 0.0)
    row_ids = jnp.arange(LAT_DEV)
    keep_above = ((row_ids > 0) | top_keep)[:, None, None]
    keep_below = ((row_ids < LAT_DEV - 1) | bottom_keep)[:, None, None]
    highest = lax.Precision.HIGHEST
    line_cells = obs_column.reshape(line_count, OBS_BLOCK)
    line_row = line_cells[:, 0] // LON_DEV
    row_hot = (line_row[:, None] == jnp.arange(LAT_DEV, dtype=jnp.int32)[None, :]).astype(
        jnp.float32
    )
    col_hot = (
        (line_cells % LON_DEV)[:, :, None] == jnp.arange(LON_DEV, dtype=jnp.int32)[None, None, :]
    ).astype(jnp.float32)
    jac_lines = jacobian.reshape(line_count, OBS_BLOCK, LEV).astype(jnp.float32)
    block_hot = (
        (obs_channel // CH_BLOCK)[:, None] == jnp.arange(block_ids, dtype=jnp.int32)[None, :]
    ).astype(jnp.float32)
    inner_hot = (
        (obs_channel % CH_BLOCK)[:, None] == jnp.arange(CH_BLOCK, dtype=jnp.int32)[None, :]
    ).astype(jnp.float32)

    def smooth_local(state_field):
        padded = with_halo(state_field, (("swath", 0), ("chan", 1)), 1)
        above_row = jnp.where(keep_above, padded[:-2, 1:-1], 0.0)
        below_row = jnp.where(keep_below, padded[2:, 1:-1], 0.0)
        beside = above_row + below_row + padded[1:-1, :-2] + padded[1:-1, 2:]
        return state_field + smoothing * (beside - 4.0 * state_field)

    def adjoint(values):
        terms = jac_lines * values.reshape(line_count, OBS_BLOCK)[:, :, None]
        line_fields = jnp.einsum("box,bok->bxk", col_hot, terms, precision=highest)
        return jnp.einsum("bl,bxk->lxk", row_hot, line_fields, precision=highest)

    def partial_table(terms):
        rows_in = terms.shape[0]
        spread = (terms[:, None, :] * block_hot.T[None, :, :]).reshape(
            rows_in * block_ids, slot_total
        )
        table = jnp.dot(spread, inner_hot, precision=highest)
        return table.reshape(rows_in, channels_all)

    def to_owners(partial_value):
        owned = lax.psum_scatter(partial_value, "chan", scatter_dimension=1, tiled=True)
        return lax.psum(owned, "swath")

    def inner(state_one, state_two, bias_one, bias_two):
        return jnp.sum(state_one * state_two) + bias_weight * jnp.sum(bias_one * bias_two)

    source = weights * innovations
    stacked = to_owners(
        partial_table(
            jnp.concatenate(
                [predictors * source[None, :], predictors * predictors * weights[None, :]], axis=0
            )
        )
    )
    res_state = smooth_local(adjoint(source))
    res_bias = stacked[:NPRED]
    diagonal = bias_precision + stacked[NPRED:]
    sol_state = jnp.zeros_like(res_state)
    sol_bias = jnp.zeros_like(res_bias)
    pre_bias = res_bias / diagonal
    record = []

    def norms_of(state_res, bias_res, bias_pre):
        return lax.psum(
            (
                inner(state_res, state_res, bias_res, bias_pre),
                inner(state_res, state_res, bias_res, bias_res),
            ),
            ("swath", "chan"),
        )

    rz_now, rr_now = norms_of(res_state, res_bias, pre_bias)
    record.append(rr_now)
    dir_state, dir_bias = (res_state, pre_bias)
    for turn_index in range(ITERS):
        smoothed = smooth_local(dir_state)
        hessian_everything = lax.all_gather(dir_bias, "chan", axis=1, tiled=True)
        flat = hessian_everything.reshape(NPRED * block_ids, CH_BLOCK)
        mid = jnp.dot(inner_hot, flat.T, precision=highest).reshape(slot_total, NPRED, block_ids)
        looked = jnp.sum(mid * predictors.T[:, :, None] * block_hot[:, None, :], axis=(1, 2))
        forward_line_fields = jnp.einsum("bl,lxk->bxk", row_hot, smoothed, precision=highest)
        picked = jnp.einsum("box,bxk->bok", col_hot, forward_line_fields, precision=highest)
        image = weights * (jnp.sum(jac_lines * picked, axis=2).reshape(-1) + looked)
        state_out = dir_state + smooth_local(adjoint(image))
        bias_out = bias_precision * dir_bias + to_owners(partial_table(predictors * image[None, :]))
        curve = lax.psum(inner(dir_state, state_out, dir_bias, bias_out), ("swath", "chan"))
        length = rz_now / curve
        sol_state = sol_state + length * dir_state
        sol_bias = sol_bias + length * dir_bias
        res_state = res_state - length * state_out
        res_bias = res_bias - length * bias_out
        pre_bias = res_bias / diagonal
        rz_next, rr_now = norms_of(res_state, res_bias, pre_bias)
        record.append(rr_now)
        ratio = rz_next / rz_now
        dir_state = res_state + ratio * dir_state
        dir_bias = pre_bias + ratio * dir_bias
        rz_now = rz_next
    return (sol_state, sol_bias, jnp.sqrt(jnp.stack(record)))


def solution(mesh):
    placed = (
        P(("swath", "chan")),
        P(("swath", "chan")),
        P(("swath", "chan"), None),
        P(None, ("swath", "chan")),
        P(("swath", "chan")),
        P(("swath", "chan")),
        P("swath", "chan"),
        P(),
        P(None, "chan"),
    )
    return jax.shard_map(
        body,
        mesh=mesh,
        in_specs=placed,
        out_specs=(P("swath", "chan", None), P(None, "chan"), P()),
        check_vma=False,
    )
```

profile of v0, /device:TPU:0, one launch (start us, length us, event | category | flops | bytes accessed | tf_op | source)
XLA Modules:
  0.0 604.4 jit_solution(15087410023057047075)
XLA Ops:
  10.6 7.1 %fusion.17 = f32[128,64,128]{2,1,0:T(8,128)S(1)} fusion(bf16[128,128,128]{2,1,0:T(8,128)(2,1)} %bitcast.41, f32[128,128]{1,0:T(8,128)S(1)} %bitcast.49, s32[128,128]{1,0:T(8,128)S(1)} %add_select_fusion.2), kind=kOutput, calls=%fused_computation.21 | convolution fusion | flops 1615855616 | bytes 8519680 | tf_op jit(solution)/shard_map/box,bok->bxk/dot_general | solution.py:79
  26.0 8.5 %broadcast_multiply_fusion = f32[16,20,16384]{2,1,0:T(8,128)} fusion(f32[20,16384]{1,0:T(8,128)S(1)} %fusion.50, f32[16,16384]{1,0:T(8,128)S(1)} %pad_maximum_fusion.48), kind=kLoop, calls=%fused_computation.9 | loop fusion | flops 5242880 | bytes 23330816 | tf_op jit(solution)/shard_map/mul | solution.py:84
  38.8 17.1 %mul.337 = f32[320,16384]{1,0:T(8,128)} reshape(f32[16,20,16384]{2,1,0:T(8,128)} %broadcast_multiply_fusion) | data formatting | bytes 41943040 | tf_op jit(solution)/shard_map/mul | solution.py:84
  60.5 16.8 %fusion.5 = f32[320,256]{1,0:T(8,128)} fusion(f32[320,16384]{1,0:T(8,128)} %mul.337, s32[16384]{0:T(1024)S(1)} %get-tuple-element.55), kind=kOutput, calls=%fused_computation.8 | convolution fusion | flops 16110321664 | bytes 21364736 | tf_op jit(solution)/shard_map/dot_general | solution.py:87
  92.3 7.2 %fusion.91 = f32[128,64,128]{2,0,1:T(8,128)} fusion(f32[32,64,128]{2,0,1:T(8,128)} %copy-done.9, f32[34,1,128]{2,0,1:T(8,128)} %collective-permute-done.7, f32[1,64,128]{2,0,1:T(1,128)S(1)} %collective-permute-done.5, f32[1,64,128]{2,0,1:T(1,128)} %collective-permute-done.4, f32[34,1,128]{2,0,1:T(8,128)} %collective-permute-done.6, f32[128]{0:T(128)S(1)} %copy-done.31, ...), kind=kOutput, calls=%fused_computation.113 | convolution fusion | flops 407113728 | bytes 5344320 | tf_op jit(solution)/shard_map/bl,lxk->bxk/dot_general | solution.py:131
  101.3 11.4 %multiply_reduce_fusion.1 = f32[128,128]{1,0:T(8,128)S(1)} fusion(f32[128,128,128]{1,2,0:T(8,128)} %copy.21, f32[128,64,128]{2,0,1:T(8,128)} %fusion.91, s32[128,128]{1,0:T(8,128)S(1)} %add_select_fusion.2), kind=kOutput, calls=%fused_computation.15 | convolution fusion | flops 1615839232 | bytes 12713984 | tf_op jit(solution)/shard_map/box,bxk->bok/dot_general | solution.py:132
  112.7 40.4 %all-reduce.4.cloned.1.call-done = f32[16,1280]{1,0:T(8,128)} async-done(((f32[16,1280]{1,0:T(8,128)}), f32[16,1280]{1,0:T(8,128)}) %all-reduce.4.cloned.1.call-update) | async-done | bytes 81936 | tf_op jit(solution)/shard_map/psum | solution.py:92
  153.9 14.0 %all_gather.6 = f32[8,5120]{1,0:T(8,128)S(1)} all-gather(f32[8,1280]{1,0:T(8,128)S(1)} %slice_divide_fusion), channel_id=1, replica_groups=mesh['swath'=8,'chan'=4] {'chan'}, dimensions={1}, use_global_device_ids=true | all-gather | bytes 204800 | tf_op jit(solution)/shard_map/all_gather | solution.py:127
  167.9 12.2 %fusion.35 = f32[16384]{0:T(1024)S(1)} fusion(f32[16384,20]{0,1:T(8,128)} %fusion.51, f32[16384,8]{0,1:T(8,128)S(1)} %bitcast.45, s32[16384]{0:T(1024)S(1)} %get-tuple-element.55, f32[8,20,256]{2,0,1:T(8,128)S(1)} %bitcast.52), kind=kOutput, calls=%fused_computation.42 | convolution fusion | flops 8065105920 | bytes 2129920 | tf_op jit(solution)/shard_map/dot_general | solution.py:129
  198.1 8.7 %mul.360 = f32[160,16384]{1,0:T(8,128)} reshape(f32[8,20,16384]{2,1,0:T(8,128)} %broadcast_multiply_fusion.2) | data formatting | bytes 20971520 | tf_op jit(solution)/shard_map/mul | solution.py:84
  212.0 11.9 %fusion.3 = f32[160,256]{1,0:T(8,128)} fusion(f32[160,16384]{1,0:T(8,128)} %mul.360, s32[16384]{0:T(1024)S(1)} %get-tuple-element.55), kind=kOutput, calls=%fused_computation.6 | convolution fusion | flops 8057257984 | bytes 10715136 | tf_op jit(solution)/shard_map/dot_general | solution.py:87
  232.6 13.9 %reduce-scatter.6.cloned.1.call-done = f32[8,1280]{1,0:T(8,128)} async-done(((f32[8,5120]{1,0:T(8,128)}), f32[8,1280]{1,0:T(8,128)}) %reduce-scatter.6.cloned.1.call-update) | async-done | bytes 40976 | tf_op jit(solution)/shard_map/reduce_scatter | solution.py:91
  246.5 23.9 %psum.72 = f32[8,1280]{1,0:T(8,128)} all-reduce(f32[8,1280]{1,0:T(8,128)} %reduce-scatter.6.cloned.1.call-done), channel_id=1, replica_groups=mesh['swath'=8,'chan'=4] {'swath'}, use_global_device_ids=true, to_apply=%region_9.10 | all-reduce | flops 10240 | bytes 81920 | tf_op jit(solution)/shard_map/psum | solution.py:92
  274.5 37.6 %all-reduce.1 = (f32[]{:T(128)}, f32[]{:T(128)}) all-reduce(f32[]{:T(128)S(6)} %add.166, f32[]{:T(128)S(6)} %add.178), channel_id=1, replica_groups=mesh['swath'=8,'chan'=4] {'swath','chan'}, use_global_device_ids=true, to_apply=%region_4.5 | all-reduce | flops 2 | bytes 16 | tf_op jit(solution)/shard_map/psum | solution.py:114
  319.4 42.3 %psum.74 = f32[]{:T(128)} all-reduce(f32[]{:T(128)S(6)} %add.179), channel_id=1, replica_groups=mesh['swath'=8,'chan'=4] {'swath','chan'}, use_global_device_ids=true, to_apply=%region_14.15 | all-reduce | flops 1 | bytes 8 | tf_op jit(solution)/shard_map/psum | solution.py:114
  367.1 13.7 %all_gather.7 = f32[8,5120]{1,0:T(8,128)S(1)} all-gather(f32[8,1280]{1,0:T(8,128)S(1)} %multiply_add_fusion.4), channel_id=1, replica_groups=mesh['swath'=8,'chan'=4] {'chan'}, dimensions={1}, use_global_device_ids=true | all-gather | bytes 204800 | tf_op jit(solution)/shard_map/all_gather | solution.py:127
  384.1 11.7 %fusion.38 = f32[16384]{0:T(1024)} fusion(f32[16384,20]{0,1:T(8,128)S(1)} %copy-done.10, f32[16384,8]{0,1:T(8,128)S(1)} %bitcast.46, s32[16384]{0:T(1024)S(1)} %get-tuple-element.55, f32[8,20,256]{2,0,1:T(8,128)S(1)} %bitcast.51), kind=kOutput, calls=%fused_computation.43 | convolution fusion | flops 8065105920 | bytes 2129920 | tf_op jit(solution)/shard_map/dot_general | solution.py:129
  401.8 11.9 %multiply_reduce_fusion = f32[128,128]{1,0:T(8,128)S(1)} fusion(f32[128,128,128]{1,2,0:T(8,128)} %copy.21, f32[128,64,128]{2,0,1:T(8,128)S(1)} %fusion.65, s32[128,128]{1,0:T(8,128)S(1)} %add_select_fusion.2), kind=kOutput, calls=%fused_computation.12 | convolution fusion | flops 1615839232 | bytes 12713984 | tf_op jit(solution)/shard_map/box,bxk->bok/dot_general | solution.py:132
  431.1 8.8 %mul.392 = f32[160,16384]{1,0:T(8,128)} reshape(f32[8,20,16384]{2,1,0:T(8,128)} %broadcast_multiply_fusion.1) | data formatting | bytes 20971520 | tf_op jit(solution)/shard_map/mul | solution.py:84
  444.3 12.0 %fusion.2 = f32[160,256]{1,0:T(8,128)} fusion(f32[160,16384]{1,0:T(8,128)} %mul.392, s32[16384]{0:T(1024)S(1)} %get-tuple-element.55), kind=kOutput, calls=%fused_computation.5 | convolution fusion | flops 8057257984 | bytes 10715136 | tf_op jit(solution)/shard_map/dot_general | solution.py:87
  463.7 15.0 %reduce-scatter.8.cloned.1.call-done = f32[8,1280]{1,0:T(8,128)} async-done(((f32[8,5120]{1,0:T(8,128)}), f32[8,1280]{1,0:T(8,128)}) %reduce-scatter.8.cloned.1.call-update) | async-done | bytes 40976 | tf_op jit(solution)/shard_map/reduce_scatter | solution.py:91
  478.7 23.3 %psum.75 = f32[8,1280]{1,0:T(8,128)S(1)} all-reduce(f32[8,1280]{1,0:T(8,128)} %reduce-scatter.8.cloned.1.call-done), channel_id=1, replica_groups=mesh['swath'=8,'chan'=4] {'swath'}, use_global_device_ids=true, to_apply=%region_19.20 | all-reduce | flops 10240 | bytes 81920 | tf_op jit(solution)/shard_map/psum | solution.py:92
  504.4 37.5 %psum.76 = f32[]{:T(128)} all-reduce(f32[]{:T(128)S(6)} %add.193), channel_id=1, replica_groups=mesh['swath'=8,'chan'=4] {'swath','chan'}, use_global_device_ids=true, to_apply=%region_21.22 | all-reduce | flops 1 | bytes 8 | tf_op jit(solution)/shard_map/psum | solution.py:136
  551.5 43.7 %all-reduce = (f32[1]{0:T(128)}, f32[1]{0:T(128)}, f32[1]{0:T(128)}) all-reduce(f32[1]{0:T(128)} %bitcast.16, f32[1]{0:T(128)} %bitcast.15, f32[1]{0:T(128)} %bitcast.14), channel_id=1, replica_groups=mesh['swath'=8,'chan'=4] {'swath','chan'}, use_global_device_ids=true, to_apply=%region_28.29 | all-reduce | flops 3 | bytes 24 | tf_op jit(solution)/shard_map/psum | solution.py:114
  (174 shorter events, 125.3 us)
Async XLA Ops:
  7.2 94.0 %reduce-scatter.4.cloned.1.call-start = ((), (), s32[]{:S(2)}) async-start(), calls=%async_computation.3 | async-start | bytes 409600 | tf_op jit(solution)/shard_map/reduce_scatter | solution.py:91
  22.3 12.2 %collective-permute-start.1 = (f32[1,64,128]{2,0,1:T(1,128)}, f32[1,64,128]{2,0,1:T(1,128)S(1)}, u32[]{:S(2)}, u32[]{:S(2)}) collective-permute-start(f32[1,64,128]{2,0,1:T(1,128)} %get-tuple-element.52), channel_id=1, source_target_pairs={{4,0},{8,4},{12,8},{16,12},{20,16},{24,20},{28,24},{0,28},{5,1},{9... | collective-permute-start | bytes 98312 | tf_op jit(solution)/shard_map/ppermute | solution.py:23
  25.7 8.9 %collective-permute-start = (f32[1,64,128]{2,0,1:T(1,128)}, f32[1,64,128]{2,0,1:T(1,128)S(1)}, u32[]{:S(2)}, u32[]{:S(2)}) collective-permute-start(f32[1,64,128]{2,0,1:T(1,128)} %get-tuple-element.51), channel_id=1, source_target_pairs={{0,4},{4,8},{8,12},{12,16},{16,20},{20,24},{24,28},{28,0},{1,5},{5... | collective-permute-start | bytes 98312 | tf_op jit(solution)/shard_map/ppermute | solution.py:22
  35.2 20.7 %collective-permute-start.3 = (f32[34,1,128]{2,0,1:T(8,128)}, f32[34,1,128]{2,0,1:T(8,128)S(1)}, u32[]{:S(2)}, u32[]{:S(2)}) collective-permute-start(f32[34,1,128]{2,0,1:T(8,128)} %get-tuple-element.40), channel_id=1, source_target_pairs={{1,0},{2,1},{3,2},{0,3},{5,4},{6,5},{7,6},{4,7},{9,8},{10,9},{11,1... | collective-permute-start | bytes 52232 | tf_op jit(solution)/shard_map/ppermute | solution.py:23
  38.8 17.1 %collective-permute-start.2 = (f32[34,1,128]{2,0,1:T(8,128)S(1)}, f32[34,1,128]{2,0,1:T(8,128)S(1)}, u32[]{:S(2)}, u32[]{:S(2)}) collective-permute-start(f32[34,1,128]{2,0,1:T(8,128)S(1)} %get-tuple-element.39), channel_id=1, source_target_pairs={{0,1},{1,2},{2,3},{3,0},{4,5},{5,6},{6,7},{7,4},{8,9},{9,10},{10,1... | collective-permute-start | bytes 52232 | tf_op jit(solution)/shard_map/ppermute | solution.py:22
  58.1 21.1 %collective-permute-start.5 = (f32[1,64,128]{2,0,1:T(1,128)}, f32[1,64,128]{2,0,1:T(1,128)S(1)}, u32[]{:S(2)}, u32[]{:S(2)}) collective-permute-start(f32[1,64,128]{2,0,1:T(1,128)} %get-tuple-element.50), channel_id=1, source_target_pairs={{4,0},{8,4},{12,8},{16,12},{20,16},{24,20},{28,24},{0,28},{5,1},{9... | collective-permute-start | bytes 98312 | tf_op jit(solution)/shard_map/ppermute | solution.py:23
  60.5 18.7 %collective-permute-start.4 = (f32[1,64,128]{2,0,1:T(1,128)}, f32[1,64,128]{2,0,1:T(1,128)}, u32[]{:S(2)}, u32[]{:S(2)}) collective-permute-start(f32[1,64,128]{2,0,1:T(1,128)} %get-tuple-element.49), channel_id=1, source_target_pairs={{0,4},{4,8},{8,12},{12,16},{16,20},{20,24},{24,28},{28,0},{1,5},{5... | collective-permute-start | bytes 98312 | tf_op jit(solution)/shard_map/ppermute | solution.py:22
  79.1 74.0 %all-reduce.4.cloned.1.call-start = ((), (), s32[]{:S(2)}) async-start(), calls=%async_computation.4 | async-start | bytes 163840 | tf_op jit(solution)/shard_map/psum | solution.py:92
  79.9 12.3 %collective-permute-start.7 = (f32[34,1,128]{2,0,1:T(8,128)S(1)}, f32[34,1,128]{2,0,1:T(8,128)}, u32[]{:S(2)}, u32[]{:S(2)}) collective-permute-start(f32[34,1,128]{2,0,1:T(8,128)S(1)} %get-tuple-element.38), channel_id=1, source_target_pairs={{1,0},{2,1},{3,2},{0,3},{5,4},{6,5},{7,6},{4,7},{9,8},{10,9},{11,1... | collective-permute-start | bytes 52232 | tf_op jit(solution)/shard_map/ppermute | solution.py:23
  83.5 8.7 %collective-permute-start.6 = (f32[34,1,128]{2,0,1:T(8,128)S(1)}, f32[34,1,128]{2,0,1:T(8,128)}, u32[]{:S(2)}, u32[]{:S(2)}) collective-permute-start(f32[34,1,128]{2,0,1:T(8,128)S(1)} %get-tuple-element.37), channel_id=1, source_target_pairs={{0,1},{1,2},{2,3},{3,0},{4,5},{5,6},{6,7},{7,4},{8,9},{9,10},{10,1... | collective-permute-start | bytes 52232 | tf_op jit(solution)/shard_map/ppermute | solution.py:22
  101.2 145.2 %reduce-scatter.6.cloned.1.call-start = ((), (), s32[]{:S(2)}) async-start(), calls=%async_computation.5 | async-start | bytes 204800 | tf_op jit(solution)/shard_map/reduce_scatter | solution.py:91
  191.7 15.1 %collective-permute-start.9 = (f32[1,64,128]{2,0,1:T(1,128)}, f32[1,64,128]{2,0,1:T(1,128)S(1)}, u32[]{:S(2)}, u32[]{:S(2)}) collective-permute-start(f32[1,64,128]{2,0,1:T(1,128)} %get-tuple-element.48), channel_id=1, source_target_pairs={{4,0},{8,4},{12,8},{16,12},{20,16},{24,20},{28,24},{0,28},{5,1},{9... | collective-permute-start | bytes 98312 | tf_op jit(solution)/shard_map/ppermute | solution.py:23
  191.7 15.1 %collective-permute-start.8 = (f32[1,64,128]{2,0,1:T(1,128)}, f32[1,64,128]{2,0,1:T(1,128)S(1)}, u32[]{:S(2)}, u32[]{:S(2)}) collective-permute-start(f32[1,64,128]{2,0,1:T(1,128)} %get-tuple-element.47), channel_id=1, source_target_pairs={{0,4},{4,8},{8,12},{12,16},{16,20},{20,24},{24,28},{28,0},{1,5},{5... | collective-permute-start | bytes 98312 | tf_op jit(solution)/shard_map/ppermute | solution.py:22
  208.3 17.4 %collective-permute-start.11 = (f32[34,1,128]{2,0,1:T(8,128)}, f32[34,1,128]{2,0,1:T(8,128)}, u32[]{:S(2)}, u32[]{:S(2)}) collective-permute-start(f32[34,1,128]{2,0,1:T(8,128)} %get-tuple-element.36), channel_id=1, source_target_pairs={{1,0},{2,1},{3,2},{0,3},{5,4},{6,5},{7,6},{4,7},{9,8},{10,9},{11,1... | collective-permute-start | bytes 52232 | tf_op jit(solution)/shard_map/ppermute | solution.py:23
  211.8 13.9 %collective-permute-start.10 = (f32[34,1,128]{2,0,1:T(8,128)}, f32[34,1,128]{2,0,1:T(8,128)}, u32[]{:S(2)}, u32[]{:S(2)}) collective-permute-start(f32[34,1,128]{2,0,1:T(8,128)} %get-tuple-element.35), channel_id=1, source_target_pairs={{0,1},{1,2},{2,3},{3,0},{4,5},{5,6},{6,7},{7,4},{8,9},{9,10},{10,1... | collective-permute-start | bytes 52232 | tf_op jit(solution)/shard_map/ppermute | solution.py:22
  225.6 253.1 %reduce-scatter.8.cloned.1.call-start = ((), (), s32[]{:S(2)}) async-start(), calls=%async_computation.6 | async-start | bytes 204800 | tf_op jit(solution)/shard_map/reduce_scatter | solution.py:91
  365.1 15.7 %collective-permute-start.13 = (f32[1,64,128]{2,0,1:T(1,128)S(1)}, f32[1,64,128]{2,0,1:T(1,128)S(1)}, u32[]{:S(2)}, u32[]{:S(2)}) collective-permute-start(f32[1,64,128]{2,0,1:T(1,128)S(1)} %get-tuple-element.46), channel_id=1, source_target_pairs={{4,0},{8,4},{12,8},{16,12},{20,16},{24,20},{28,24},{0,28},{5,1},{9... | collective-permute-start | bytes 98312 | tf_op jit(solution)/shard_map/ppermute | solution.py:23
  366.3 14.5 %collective-permute-start.12 = (f32[1,64,128]{2,0,1:T(1,128)S(1)}, f32[1,64,128]{2,0,1:T(1,128)S(1)}, u32[]{:S(2)}, u32[]{:S(2)}) collective-permute-start(f32[1,64,128]{2,0,1:T(1,128)S(1)} %get-tuple-element.45), channel_id=1, source_target_pairs={{0,4},{4,8},{8,12},{12,16},{16,20},{20,24},{24,28},{28,0},{1,5},{5... | collective-permute-start | bytes 98312 | tf_op jit(solution)/shard_map/ppermute | solution.py:22
  382.1 14.4 %collective-permute-start.15 = (f32[34,1,128]{2,0,1:T(8,128)}, f32[34,1,128]{2,0,1:T(8,128)}, u32[]{:S(2)}, u32[]{:S(2)}) collective-permute-start(f32[34,1,128]{2,0,1:T(8,128)} %get-tuple-element.34), channel_id=1, source_target_pairs={{1,0},{2,1},{3,2},{0,3},{5,4},{6,5},{7,6},{4,7},{9,8},{10,9},{11,1... | collective-permute-start | bytes 52232 | tf_op jit(solution)/shard_map/ppermute | solution.py:23
  383.7 12.8 %collective-permute-start.14 = (f32[34,1,128]{2,0,1:T(8,128)}, f32[34,1,128]{2,0,1:T(8,128)}, u32[]{:S(2)}, u32[]{:S(2)}) collective-permute-start(f32[34,1,128]{2,0,1:T(8,128)} %get-tuple-element.33), channel_id=1, source_target_pairs={{0,1},{1,2},{2,3},{3,0},{4,5},{5,6},{6,7},{7,4},{8,9},{9,10},{10,1... | collective-permute-start | bytes 52232 | tf_op jit(solution)/shard_map/ppermute | solution.py:22
  424.7 15.3 %collective-permute-start.17 = (f32[1,64,128]{2,0,1:T(1,128)S(1)}, f32[1,64,128]{2,0,1:T(1,128)S(1)}, u32[]{:S(2)}, u32[]{:S(2)}) collective-permute-start(f32[1,64,128]{2,0,1:T(1,128)S(1)} %get-tuple-element.44), channel_id=1, source_target_pairs={{4,0},{8,4},{12,8},{16,12},{20,16},{24,20},{28,24},{0,28},{5,1},{9... | collective-permute-start | bytes 98312 | tf_op jit(solution)/shard_map/ppermute | solution.py:23
  424.7 15.2 %collective-permute-start.16 = (f32[1,64,128]{2,0,1:T(1,128)S(1)}, f32[1,64,128]{2,0,1:T(1,128)S(1)}, u32[]{:S(2)}, u32[]{:S(2)}) collective-permute-start(f32[1,64,128]{2,0,1:T(1,128)S(1)} %get-tuple-element.43), channel_id=1, source_target_pairs={{0,4},{4,8},{8,12},{12,16},{16,20},{20,24},{24,28},{28,0},{1,5},{5... | collective-permute-start | bytes 98312 | tf_op jit(solution)/shard_map/ppermute | solution.py:22
  440.6 17.4 %collective-permute-start.19 = (f32[34,1,128]{2,0,1:T(8,128)}, f32[34,1,128]{2,0,1:T(8,128)S(1)}, u32[]{:S(2)}, u32[]{:S(2)}) collective-permute-start(f32[34,1,128]{2,0,1:T(8,128)} %get-tuple-element.32), channel_id=1, source_target_pairs={{1,0},{2,1},{3,2},{0,3},{5,4},{6,5},{7,6},{4,7},{9,8},{10,9},{11,1... | collective-permute-start | bytes 52232 | tf_op jit(solution)/shard_map/ppermute | solution.py:23
  444.0 14.0 %collective-permute-start.18 = (f32[34,1,128]{2,0,1:T(8,128)}, f32[34,1,128]{2,0,1:T(8,128)}, u32[]{:S(2)}, u32[]{:S(2)}) collective-permute-start(f32[34,1,128]{2,0,1:T(8,128)} %get-tuple-element.31), channel_id=1, source_target_pairs={{0,1},{1,2},{2,3},{3,0},{4,5},{5,6},{6,7},{7,4},{8,9},{9,10},{10,1... | collective-permute-start | bytes 52232 | tf_op jit(solution)/shard_map/ppermute | solution.py:22
  (38 other events, 771.6 us)
Sparse Core Ops, SparseCore 0:
  79.2 21.9 reduce-scatter.3
  104.3 48.7 all-reduce.3
  225.8 20.6 reduce-scatter.5
  458.2 20.4 reduce-scatter.7
where the time goes:
time: 613 us; the launch traced here: 604 us
  blocking collectives  236 us (38%)
  matrix products  131 us (21%)
  waiting for transfers between devices  71.1 us (12%)
  other arithmetic  58.5 us (10%)
  local copies, waits for them, and re-layouts  54.1 us (9%)
  between operations  28.4 us (5%)
  starting transfers between devices  25.2 us (4%)
    psum x3, blocking collectives, norms_of(): lax.psum((inner(state_res, state_res, bias_res, bias_pre), inner(state_re...  124 us
    psum x2, blocking collectives, to_owners(): return lax.psum(owned, 'swath')  47.2 us
    dot_general x3, matrix products, partial_table(): table = jnp.dot(spread, inner_hot, precision=highest)  40.8 us
    psum x1, waiting for transfers between devices, to_owners(): return lax.psum(owned, 'swath')  40.4 us
    psum x1, blocking collectives, body(): lax.psum(inner(dir_state, state_out, dir_bias, bias_out), ('swath', 'chan'))  37.5 us
    mul x3, local copies, waits for them, and re-layouts, partial_table(): terms[:, None, :] * block_hot.T[None, :, :]  34.6 us
    reduce_scatter x3, waiting for transfers between devices, to_owners(): lax.psum_scatter(partial_value, 'chan', scatter_dimension=1, tiled=True)  30.6 us
    all_gather x2, blocking collectives, body(): hessian_everything = lax.all_gather(dir_bias, 'chan', axis=1, tiled=True)  27.7 us
  transfers between devices with their start and end apart: 24, of which 4 were waited for; matrix products, arithmetic and copies ran while one was open for 25% of the time, Pallas kernels for 0%

commit v1 on v0

--- a/solution.py
+++ b/solution.py
@@ -89,7 +89,7 @@
 
     def to_owners(partial_value):
         owned = lax.psum_scatter(partial_value, "chan", scatter_dimension=1, tiled=True)
-        return lax.psum(owned, "swath")
+        return jnp.sum(lax.all_gather(owned, "swath"), axis=0)
 
     def inner(state_one, state_two, bias_one, bias_two):
         return jnp.sum(state_one * state_two) + bias_weight * jnp.sum(bias_one * bias_two)

time: 613 us -> 552 us (0.900)
  waiting for transfers between devices: 71.1 us -> 29 us
  blocking collectives: 236 us -> 219 us
    psum x2 -> x0, blocking collectives: 47.2 us -> none  [to_owners(): return lax.psum(owned, 'swath')]
    psum x1 -> x0, waiting for transfers between devices: 40.4 us -> none  [to_owners(): return lax.psum(owned, 'swath')]
    all_gather x0 -> x3, blocking collectives: none -> 30.8 us  [to_owners(): return jnp.sum(lax.all_gather(owned, 'swath'), axis=0)]
  transfers between devices with their start and end apart: 24 -> 23, of which waited for: 4 -> 2; matrix products, arithmetic and copies ran while one was open for 25% -> 28% of each run, Pallas kernels for 0% -> 0%
where the time goes in v1:
time: 552 us; the launch traced here: 544 us
  blocking collectives  219 us (40%)
  matrix products  130 us (24%)
  other arithmetic  57.7 us (10%)
  local copies, waits for them, and re-layouts  54.6 us (10%)
  waiting for transfers between devices  29 us (5%)
  between operations  28.1 us (5%)
  starting transfers between devices  25.5 us (5%)
    psum x3, blocking collectives, norms_of(): lax.psum((inner(state_res, state_res, bias_res, bias_pre), inner(state_re...  123 us
    dot_general x3, matrix products, partial_table(): table = jnp.dot(spread, inner_hot, precision=highest)  40.9 us
    psum x1, blocking collectives, body(): lax.psum(inner(dir_state, state_out, dir_bias, bias_out), ('swath', 'chan'))  37.5 us
    mul x3, local copies, waits for them, and re-layouts, partial_table(): terms[:, None, :] * block_hot.T[None, :, :]  34.6 us
    all_gather x3, blocking collectives, to_owners(): return jnp.sum(lax.all_gather(owned, 'swath'), axis=0)  30.8 us
    reduce_scatter x3, waiting for transfers between devices, to_owners(): lax.psum_scatter(partial_value, 'chan', scatter_dimension=1, tiled=True)  28.9 us
    all_gather x2, blocking collectives, body(): hessian_everything = lax.all_gather(dir_bias, 'chan', axis=1, tiled=True)  27.5 us
    dot_general x2, matrix products, body(): jnp.einsum('box,bxk->bok', col_hot, forward_line_fields, precision=highest)  24.2 us
  transfers between devices with their start and end apart: 23, of which 2 were waited for; matrix products, arithmetic and copies ran while one was open for 28% of the time, Pallas kernels for 0%

profile of v1, /device:TPU:0, one launch (start us, length us, event | category | flops | bytes accessed | tf_op | source)
XLA Modules:
  0.0 543.7 jit_solution(484203292477447516)
XLA Ops:
  10.6 7.1 %fusion.17 = f32[128,64,128]{2,1,0:T(8,128)S(1)} fusion(bf16[128,128,128]{2,1,0:T(8,128)(2,1)} %bitcast.46, f32[128,128]{1,0:T(8,128)S(1)} %bitcast.55, s32[128,128]{1,0:T(8,128)S(1)} %add_select_fusion.2), kind=kOutput, calls=%fused_computation.21 | convolution fusion | flops 1615855616 | bytes 8519680 | tf_op jit(solution)/shard_map/box,bok->bxk/dot_general | solution.py:79
  26.6 8.5 %broadcast_multiply_fusion = f32[16,20,16384]{2,1,0:T(8,128)} fusion(f32[20,16384]{1,0:T(8,128)S(1)} %fusion.50, f32[16,16384]{1,0:T(8,128)S(1)} %pad_maximum_fusion.48), kind=kLoop, calls=%fused_computation.9 | loop fusion | flops 5242880 | bytes 23330816 | tf_op jit(solution)/shard_map/mul | solution.py:84
  38.8 17.1 %mul.337 = f32[320,16384]{1,0:T(8,128)} reshape(f32[16,20,16384]{2,1,0:T(8,128)} %broadcast_multiply_fusion) | data formatting | bytes 41943040 | tf_op jit(solution)/shard_map/mul | solution.py:84
  60.5 16.9 %fusion.5 = f32[320,256]{1,0:T(8,128)} fusion(f32[320,16384]{1,0:T(8,128)} %mul.337, s32[16384]{0:T(1024)S(1)} %get-tuple-element.55), kind=kOutput, calls=%fused_computation.8 | convolution fusion | flops 16110321664 | bytes 21364736 | tf_op jit(solution)/shard_map/dot_general | solution.py:87
  85.8 7.0 %copy.21 = f32[128,128,128]{1,2,0:T(8,128)} copy(bf16[128,128,128]{2,1,0:T(8,128)(2,1)} %bitcast.47) | data formatting | bytes 12582912 | tf_op jit(solution)/shard_map/convert_element_type | solution.py:62
  98.1 12.3 %multiply_reduce_fusion.1 = f32[128,128]{1,0:T(8,128)} fusion(f32[128,128,128]{1,2,0:T(8,128)} %copy.21, f32[128,64,128]{2,0,1:T(8,128)S(1)} %fusion.91, s32[128,128]{1,0:T(8,128)S(1)} %add_select_fusion.2), kind=kOutput, calls=%fused_computation.15 | convolution fusion | flops 1615839232 | bytes 12713984 | tf_op jit(solution)/shard_map/box,bxk->bok/dot_general | solution.py:132
  110.4 11.7 %all-gather = f32[128,1280]{1,0:T(8,128)} all-gather(f32[16,1280]{1,0:T(8,128)} %reduce-scatter.4.cloned.1.call-done), channel_id=2, replica_groups=mesh['swath'=8,'chan'=4] {'swath'}, dimensions={0}, use_global_device_ids=true | all-gather | bytes 737280 | tf_op jit(solution)/shard_map/all_gather | solution.py:92
  123.3 13.8 %all_gather.26 = f32[8,5120]{1,0:T(8,128)S(1)} all-gather(f32[8,1280]{1,0:T(8,128)S(1)} %slice_divide_fusion), channel_id=1, replica_groups=mesh['swath'=8,'chan'=4] {'chan'}, dimensions={1}, use_global_device_ids=true | all-gather | bytes 204800 | tf_op jit(solution)/shard_map/all_gather | solution.py:127
  137.1 12.2 %fusion.35 = f32[16384]{0:T(1024)S(1)} fusion(f32[16384,20]{0,1:T(8,128)} %fusion.51, f32[16384,8]{0,1:T(8,128)S(1)} %bitcast.50, s32[16384]{0:T(1024)S(1)} %get-tuple-element.55, f32[8,20,256]{2,0,1:T(8,128)S(1)} %bitcast.58), kind=kOutput, calls=%fused_computation.42 | convolution fusion | flops 8065105920 | bytes 2129920 | tf_op jit(solution)/shard_map/dot_general | solution.py:129
  167.3 8.7 %mul.360 = f32[160,16384]{1,0:T(8,128)} reshape(f32[8,20,16384]{2,1,0:T(8,128)} %broadcast_multiply_fusion.2) | data formatting | bytes 20971520 | tf_op jit(solution)/shard_map/mul | solution.py:84
  181.5 11.9 %fusion.3 = f32[160,256]{1,0:T(8,128)} fusion(f32[160,16384]{1,0:T(8,128)} %mul.360, s32[16384]{0:T(1024)S(1)} %get-tuple-element.55), kind=kOutput, calls=%fused_computation.6 | convolution fusion | flops 8057257984 | bytes 10715136 | tf_op jit(solution)/shard_map/dot_general | solution.py:87
  202.0 13.5 %reduce-scatter.6.cloned.1.call-done = f32[8,1280]{1,0:T(8,128)} async-done(((f32[8,5120]{1,0:T(8,128)}), f32[8,1280]{1,0:T(8,128)}) %reduce-scatter.6.cloned.1.call-update) | async-done | bytes 40976 | tf_op jit(solution)/shard_map/reduce_scatter | solution.py:91
  215.4 9.6 %all-gather.1 = f32[64,1280]{1,0:T(8,128)S(1)} all-gather(f32[8,1280]{1,0:T(8,128)} %reduce-scatter.6.cloned.1.call-done), channel_id=3, replica_groups=mesh['swath'=8,'chan'=4] {'swath'}, dimensions={0}, use_global_device_ids=true | all-gather | bytes 368640 | tf_op jit(solution)/shard_map/all_gather | solution.py:92
  228.7 37.5 %all-reduce.1 = (f32[]{:T(128)}, f32[]{:T(128)}) all-reduce(f32[]{:T(128)S(6)} %add.160, f32[]{:T(128)S(6)} %add.172), channel_id=1, replica_groups=mesh['swath'=8,'chan'=4] {'swath','chan'}, use_global_device_ids=true, to_apply=%region_4.5 | all-reduce | flops 2 | bytes 16 | tf_op jit(solution)/shard_map/psum | solution.py:114
  273.5 41.9 %psum.51 = f32[]{:T(128)} all-reduce(f32[]{:T(128)S(6)} %add.173), channel_id=1, replica_groups=mesh['swath'=8,'chan'=4] {'swath','chan'}, use_global_device_ids=true, to_apply=%region_14.15 | all-reduce | flops 1 | bytes 8 | tf_op jit(solution)/shard_map/psum | solution.py:114
  320.8 13.7 %all_gather.29 = f32[8,5120]{1,0:T(8,128)S(1)} all-gather(f32[8,1280]{1,0:T(8,128)S(1)} %multiply_add_fusion.4), channel_id=1, replica_groups=mesh['swath'=8,'chan'=4] {'chan'}, dimensions={1}, use_global_device_ids=true | all-gather | bytes 204800 | tf_op jit(solution)/shard_map/all_gather | solution.py:127
  337.2 11.7 %fusion.38 = f32[16384]{0:T(1024)} fusion(f32[16384,20]{0,1:T(8,128)S(1)} %copy-done.10, f32[16384,8]{0,1:T(8,128)S(1)} %bitcast.51, s32[16384]{0:T(1024)S(1)} %get-tuple-element.55, f32[8,20,256]{2,0,1:T(8,128)S(1)} %bitcast.57), kind=kOutput, calls=%fused_computation.43 | convolution fusion | flops 8065105920 | bytes 2129920 | tf_op jit(solution)/shard_map/dot_general | solution.py:129
  354.8 11.9 %multiply_reduce_fusion = f32[128,128]{1,0:T(8,128)S(1)} fusion(f32[128,128,128]{1,2,0:T(8,128)} %copy.21, f32[128,64,128]{2,0,1:T(8,128)S(1)} %fusion.65, s32[128,128]{1,0:T(8,128)S(1)} %add_select_fusion.2), kind=kOutput, calls=%fused_computation.12 | convolution fusion | flops 1615839232 | bytes 12713984 | tf_op jit(solution)/shard_map/box,bxk->bok/dot_general | solution.py:132
  384.1 8.8 %mul.392 = f32[160,16384]{1,0:T(8,128)} reshape(f32[8,20,16384]{2,1,0:T(8,128)} %broadcast_multiply_fusion.1) | data formatting | bytes 20971520 | tf_op jit(solution)/shard_map/mul | solution.py:84
  397.2 12.1 %fusion.2 = f32[160,256]{1,0:T(8,128)} fusion(f32[160,16384]{1,0:T(8,128)} %mul.392, s32[16384]{0:T(1024)S(1)} %get-tuple-element.55), kind=kOutput, calls=%fused_computation.5 | convolution fusion | flops 8057257984 | bytes 10715136 | tf_op jit(solution)/shard_map/dot_general | solution.py:87
  416.4 15.5 %reduce-scatter.8.cloned.1.call-done = f32[8,1280]{1,0:T(8,128)} async-done(((f32[8,5120]{1,0:T(8,128)}), f32[8,1280]{1,0:T(8,128)}) %reduce-scatter.8.cloned.1.call-update) | async-done | bytes 40976 | tf_op jit(solution)/shard_map/reduce_scatter | solution.py:91
  431.8 9.5 %all-gather.2 = f32[64,1280]{1,0:T(8,128)S(1)} all-gather(f32[8,1280]{1,0:T(8,128)} %reduce-scatter.8.cloned.1.call-done), channel_id=4, replica_groups=mesh['swath'=8,'chan'=4] {'swath'}, dimensions={0}, use_global_device_ids=true | all-gather | bytes 368640 | tf_op jit(solution)/shard_map/all_gather | solution.py:92
  443.7 37.5 %psum.52 = f32[]{:T(128)} all-reduce(f32[]{:T(128)S(6)} %add.187), channel_id=1, replica_groups=mesh['swath'=8,'chan'=4] {'swath','chan'}, use_global_device_ids=true, to_apply=%region_21.22 | all-reduce | flops 1 | bytes 8 | tf_op jit(solution)/shard_map/psum | solution.py:136
  490.8 43.6 %all-reduce = (f32[1]{0:T(128)}, f32[1]{0:T(128)}, f32[1]{0:T(128)}) all-reduce(f32[1]{0:T(128)} %bitcast.19, f32[1]{0:T(128)} %bitcast.18, f32[1]{0:T(128)} %bitcast.17), channel_id=1, replica_groups=mesh['swath'=8,'chan'=4] {'swath','chan'}, use_global_device_ids=true, to_apply=%region_28.29 | all-reduce | flops 3 | bytes 24 | tf_op jit(solution)/shard_map/psum | solution.py:114
  (161 shorter events, 121.7 us)
Async XLA Ops:
  7.2 103.3 %reduce-scatter.4.cloned.1.call-start = ((), (), s32[]{:S(2)}) async-start(), calls=%async_computation.3 | async-start | bytes 409600 | tf_op jit(solution)/shard_map/reduce_scatter | solution.py:91
  22.3 12.8 %collective-permute-start.1 = (f32[1,64,128]{2,0,1:T(1,128)}, f32[1,64,128]{2,0,1:T(1,128)S(1)}, u32[]{:S(2)}, u32[]{:S(2)}) collective-permute-start(f32[1,64,128]{2,0,1:T(1,128)} %get-tuple-element.52), channel_id=1, source_target_pairs={{4,0},{8,4},{12,8},{16,12},{20,16},{24,20},{28,24},{0,28},{5,1},{9... | collective-permute-start | bytes 98312 | tf_op jit(solution)/shard_map/ppermute | solution.py:23
  25.7 9.4 %collective-permute-start = (f32[1,64,128]{2,0,1:T(1,128)S(1)}, f32[1,64,128]{2,0,1:T(1,128)S(1)}, u32[]{:S(2)}, u32[]{:S(2)}) collective-permute-start(f32[1,64,128]{2,0,1:T(1,128)S(1)} %get-tuple-element.51), channel_id=1, source_target_pairs={{0,4},{4,8},{8,12},{12,16},{16,20},{20,24},{24,28},{28,0},{1,5},{5... | collective-permute-start | bytes 98312 | tf_op jit(solution)/shard_map/ppermute | solution.py:22
  35.1 20.8 %collective-permute-start.3 = (f32[34,1,128]{2,0,1:T(8,128)S(1)}, f32[34,1,128]{2,0,1:T(8,128)S(1)}, u32[]{:S(2)}, u32[]{:S(2)}) collective-permute-start(f32[34,1,128]{2,0,1:T(8,128)S(1)} %get-tuple-element.40), channel_id=1, source_target_pairs={{1,0},{2,1},{3,2},{0,3},{5,4},{6,5},{7,6},{4,7},{9,8},{10,9},{11,1... | collective-permute-start | bytes 52232 | tf_op jit(solution)/shard_map/ppermute | solution.py:23
  38.8 17.1 %collective-permute-start.2 = (f32[34,1,128]{2,0,1:T(8,128)S(1)}, f32[34,1,128]{2,0,1:T(8,128)S(1)}, u32[]{:S(2)}, u32[]{:S(2)}) collective-permute-start(f32[34,1,128]{2,0,1:T(8,128)S(1)} %get-tuple-element.39), channel_id=1, source_target_pairs={{0,1},{1,2},{2,3},{3,0},{4,5},{5,6},{6,7},{7,4},{8,9},{9,10},{10,1... | collective-permute-start | bytes 52232 | tf_op jit(solution)/shard_map/ppermute | solution.py:22
  55.9 214.3 %copy-start.19 = (f32[34,1,128]{2,0,1:T(8,128)}, f32[34,1,128]{2,0,1:T(8,128)S(1)}, u32[]{:S(2)}) copy-start(f32[34,1,128]{2,0,1:T(8,128)S(1)} %collective-permute-done.2) | copy-start | bytes 52228
  58.1 21.1 %collective-permute-start.5 = (f32[1,64,128]{2,0,1:T(1,128)}, f32[1,64,128]{2,0,1:T(1,128)S(1)}, u32[]{:S(2)}, u32[]{:S(2)}) collective-permute-start(f32[1,64,128]{2,0,1:T(1,128)} %get-tuple-element.50), channel_id=1, source_target_pairs={{4,0},{8,4},{12,8},{16,12},{20,16},{24,20},{28,24},{0,28},{5,1},{9... | collective-permute-start | bytes 98312 | tf_op jit(solution)/shard_map/ppermute | solution.py:23
  60.5 18.8 %collective-permute-start.4 = (f32[1,64,128]{2,0,1:T(1,128)}, f32[1,64,128]{2,0,1:T(1,128)S(1)}, u32[]{:S(2)}, u32[]{:S(2)}) collective-permute-start(f32[1,64,128]{2,0,1:T(1,128)} %get-tuple-element.49), channel_id=1, source_target_pairs={{0,4},{4,8},{8,12},{12,16},{16,20},{20,24},{24,28},{28,0},{1,5},{5... | collective-permute-start | bytes 98312 | tf_op jit(solution)/shard_map/ppermute | solution.py:22
  79.1 136.3 %reduce-scatter.6.cloned.1.call-start = ((), (), s32[]{:S(2)}) async-start(), calls=%async_computation.4 | async-start | bytes 204800 | tf_op jit(solution)/shard_map/reduce_scatter | solution.py:91
  80.6 12.3 %collective-permute-start.7 = (f32[34,1,128]{2,0,1:T(8,128)}, f32[34,1,128]{2,0,1:T(8,128)}, u32[]{:S(2)}, u32[]{:S(2)}) collective-permute-start(f32[34,1,128]{2,0,1:T(8,128)} %get-tuple-element.38), channel_id=1, source_target_pairs={{1,0},{2,1},{3,2},{0,3},{5,4},{6,5},{7,6},{4,7},{9,8},{10,9},{11,1... | collective-permute-start | bytes 52232 | tf_op jit(solution)/shard_map/ppermute | solution.py:23
  84.1 8.7 %collective-permute-start.6 = (f32[34,1,128]{2,0,1:T(8,128)}, f32[34,1,128]{2,0,1:T(8,128)}, u32[]{:S(2)}, u32[]{:S(2)}) collective-permute-start(f32[34,1,128]{2,0,1:T(8,128)} %get-tuple-element.37), channel_id=1, source_target_pairs={{0,1},{1,2},{2,3},{3,0},{4,5},{5,6},{6,7},{7,4},{8,9},{9,10},{10,1... | collective-permute-start | bytes 52232 | tf_op jit(solution)/shard_map/ppermute | solution.py:22
  160.9 15.2 %collective-permute-start.9 = (f32[1,64,128]{2,0,1:T(1,128)}, f32[1,64,128]{2,0,1:T(1,128)}, u32[]{:S(2)}, u32[]{:S(2)}) collective-permute-start(f32[1,64,128]{2,0,1:T(1,128)} %get-tuple-element.48), channel_id=1, source_target_pairs={{4,0},{8,4},{12,8},{16,12},{20,16},{24,20},{28,24},{0,28},{5,1},{9... | collective-permute-start | bytes 98312 | tf_op jit(solution)/shard_map/ppermute | solution.py:23
  160.9 15.2 %collective-permute-start.8 = (f32[1,64,128]{2,0,1:T(1,128)}, f32[1,64,128]{2,0,1:T(1,128)}, u32[]{:S(2)}, u32[]{:S(2)}) collective-permute-start(f32[1,64,128]{2,0,1:T(1,128)} %get-tuple-element.47), channel_id=1, source_target_pairs={{0,4},{4,8},{8,12},{12,16},{16,20},{20,24},{24,28},{28,0},{1,5},{5... | collective-permute-start | bytes 98312 | tf_op jit(solution)/shard_map/ppermute | solution.py:22
  177.5 17.7 %collective-permute-start.11 = (f32[34,1,128]{2,0,1:T(8,128)}, f32[34,1,128]{2,0,1:T(8,128)}, u32[]{:S(2)}, u32[]{:S(2)}) collective-permute-start(f32[34,1,128]{2,0,1:T(8,128)} %get-tuple-element.36), channel_id=1, source_target_pairs={{1,0},{2,1},{3,2},{0,3},{5,4},{6,5},{7,6},{4,7},{9,8},{10,9},{11,1... | collective-permute-start | bytes 52232 | tf_op jit(solution)/shard_map/ppermute | solution.py:23
  181.1 14.0 %collective-permute-start.10 = (f32[34,1,128]{2,0,1:T(8,128)}, f32[34,1,128]{2,0,1:T(8,128)}, u32[]{:S(2)}, u32[]{:S(2)}) collective-permute-start(f32[34,1,128]{2,0,1:T(8,128)} %get-tuple-element.35), channel_id=1, source_target_pairs={{0,1},{1,2},{2,3},{3,0},{4,5},{5,6},{6,7},{7,4},{8,9},{9,10},{10,1... | collective-permute-start | bytes 52232 | tf_op jit(solution)/shard_map/ppermute | solution.py:22
  195.1 236.7 %reduce-scatter.8.cloned.1.call-start = ((), (), s32[]{:S(2)}) async-start(), calls=%async_computation.5 | async-start | bytes 204800 | tf_op jit(solution)/shard_map/reduce_scatter | solution.py:91
  319.6 14.9 %collective-permute-start.13 = (f32[1,64,128]{2,0,1:T(1,128)S(1)}, f32[1,64,128]{2,0,1:T(1,128)S(1)}, u32[]{:S(2)}, u32[]{:S(2)}) collective-permute-start(f32[1,64,128]{2,0,1:T(1,128)S(1)} %get-tuple-element.46), channel_id=1, source_target_pairs={{4,0},{8,4},{12,8},{16,12},{20,16},{24,20},{28,24},{0,28},{5,1},{9... | collective-permute-start | bytes 98312 | tf_op jit(solution)/shard_map/ppermute | solution.py:23
  320.8 13.7 %collective-permute-start.12 = (f32[1,64,128]{2,0,1:T(1,128)S(1)}, f32[1,64,128]{2,0,1:T(1,128)S(1)}, u32[]{:S(2)}, u32[]{:S(2)}) collective-permute-start(f32[1,64,128]{2,0,1:T(1,128)S(1)} %get-tuple-element.45), channel_id=1, source_target_pairs={{0,4},{4,8},{8,12},{12,16},{16,20},{20,24},{24,28},{28,0},{1,5},{5... | collective-permute-start | bytes 98312 | tf_op jit(solution)/shard_map/ppermute | solution.py:22
  335.1 14.3 %collective-permute-start.15 = (f32[34,1,128]{2,0,1:T(8,128)}, f32[34,1,128]{2,0,1:T(8,128)}, u32[]{:S(2)}, u32[]{:S(2)}) collective-permute-start(f32[34,1,128]{2,0,1:T(8,128)} %get-tuple-element.34), channel_id=1, source_target_pairs={{1,0},{2,1},{3,2},{0,3},{5,4},{6,5},{7,6},{4,7},{9,8},{10,9},{11,1... | collective-permute-start | bytes 52232 | tf_op jit(solution)/shard_map/ppermute | solution.py:23
  336.8 12.7 %collective-permute-start.14 = (f32[34,1,128]{2,0,1:T(8,128)}, f32[34,1,128]{2,0,1:T(8,128)}, u32[]{:S(2)}, u32[]{:S(2)}) collective-permute-start(f32[34,1,128]{2,0,1:T(8,128)} %get-tuple-element.33), channel_id=1, source_target_pairs={{0,1},{1,2},{2,3},{3,0},{4,5},{5,6},{6,7},{7,4},{8,9},{9,10},{10,1... | collective-permute-start | bytes 52232 | tf_op jit(solution)/shard_map/ppermute | solution.py:22
  377.6 15.3 %collective-permute-start.17 = (f32[1,64,128]{2,0,1:T(1,128)S(1)}, f32[1,64,128]{2,0,1:T(1,128)S(1)}, u32[]{:S(2)}, u32[]{:S(2)}) collective-permute-start(f32[1,64,128]{2,0,1:T(1,128)S(1)} %get-tuple-element.44), channel_id=1, source_target_pairs={{4,0},{8,4},{12,8},{16,12},{20,16},{24,20},{28,24},{0,28},{5,1},{9... | collective-permute-start | bytes 98312 | tf_op jit(solution)/shard_map/ppermute | solution.py:23
  377.7 15.2 %collective-permute-start.16 = (f32[1,64,128]{2,0,1:T(1,128)S(1)}, f32[1,64,128]{2,0,1:T(1,128)S(1)}, u32[]{:S(2)}, u32[]{:S(2)}) collective-permute-start(f32[1,64,128]{2,0,1:T(1,128)S(1)} %get-tuple-element.43), channel_id=1, source_target_pairs={{0,4},{4,8},{8,12},{12,16},{16,20},{20,24},{24,28},{28,0},{1,5},{5... | collective-permute-start | bytes 98312 | tf_op jit(solution)/shard_map/ppermute | solution.py:22
  393.6 17.5 %collective-permute-start.19 = (f32[34,1,128]{2,0,1:T(8,128)}, f32[34,1,128]{2,0,1:T(8,128)S(1)}, u32[]{:S(2)}, u32[]{:S(2)}) collective-permute-start(f32[34,1,128]{2,0,1:T(8,128)} %get-tuple-element.32), channel_id=1, source_target_pairs={{1,0},{2,1},{3,2},{0,3},{5,4},{6,5},{7,6},{4,7},{9,8},{10,9},{11,1... | collective-permute-start | bytes 52232 | tf_op jit(solution)/shard_map/ppermute | solution.py:23
  397.0 14.0 %collective-permute-start.18 = (f32[34,1,128]{2,0,1:T(8,128)}, f32[34,1,128]{2,0,1:T(8,128)}, u32[]{:S(2)}, u32[]{:S(2)}) collective-permute-start(f32[34,1,128]{2,0,1:T(8,128)} %get-tuple-element.31), channel_id=1, source_target_pairs={{0,1},{1,2},{2,3},{3,0},{4,5},{5,6},{6,7},{7,4},{8,9},{9,10},{10,1... | collective-permute-start | bytes 52232 | tf_op jit(solution)/shard_map/ppermute | solution.py:22
  (30 other events, 873.4 us)
Sparse Core Ops, SparseCore 0:
  79.3 21.8 reduce-scatter.3
  195.2 20.1 reduce-scatter.5
  411.2 20.6 reduce-scatter.7
